TPU v7x, 32 devices: a whole 2x2x4 slice. The times are simulated.
32 devices in a mesh: rep: 2 (over x), shard: 16 (over z, y, core).
Axes of the slice: x: 2, y: 2, z: 4, core: 2. Of those that a mesh axis runs over, the one named last changes fastest.
Arguments:
- tokens: bfloat16 [2, 32, 64, 1024], P(None, ('rep', 'shard')), may hold values from -6 to 6
- prefix: int32 [2, 32], P(None, ('rep', 'shard')), may hold values from 6 to 32
- qkv_weight: bfloat16 [1024, 3072], P('shard'), may hold values from -0.1875 to 0.1875
- out_weight: bfloat16 [1024, 1024], P('shard'), may hold values from -1 to 1
- in_weight: bfloat16 [1024, 5632], P('shard'), may hold values from -0.1875 to 0.1875
- down_weight: bfloat16 [2816, 1024], P('shard'), may hold values from -0.109375 to 0.109375
- cotangent: bfloat16 [2, 32, 64, 1024], P(None, ('rep', 'shard')), may hold values from -6 to 6
Outputs:
- result: bfloat16 [2, 32, 64, 1024], P(None, ('rep', 'shard'))
- grad_tokens: float32 [2, 32, 64, 1024], P(None, ('rep', 'shard'))
- grad_qkv: float32 [1024, 3072], P('shard')
- grad_out: float32 [1024, 1024], P('shard')
- grad_in: float32 [1024, 5632], P('shard')
- grad_down: float32 [2816, 1024], P('shard')
Inputs may be any that keep to these rules, and one draw needn't show every extreme that they name: Each sequence's prefix length, a tenth to a half of 64.
All inputs are finite; a program needn't handle non-finite values.
Results may differ from a plain program's by a relative error of at most 0.014.
Values may be sent and summed in bfloat16 or wider, within the bound.
No kernel may reach another device: no remote copies, remote signals or barrier semaphores. Data moves between devices by JAX's collectives and lax.ppermute only.
A program may use at most 256 MiB of HBM per device.

v0:
```python
import jax
import jax.numpy as jnp
from jax import lax
from jax.sharding import PartitionSpec as P

H = 16
HD = 64


def norm_rows(values):
    centre = values - jnp.mean(values, axis=-1, keepdims=True)
    inverse = lax.rsqrt(jnp.mean(centre * centre, axis=-1, keepdims=True) + 1e-05)
    return (centre * inverse, inverse)


def norm_back(normed, inverse, upstream):
    return inverse * (
        upstream
        - jnp.mean(upstream, axis=-1, keepdims=True)
        - normed * jnp.mean(upstream * normed, axis=-1, keepdims=True)
    )


def rope_tables(length, head_size):
    position = jnp.arange(length, dtype=jnp.float32)[:, None]
    frequency = 10000.0 ** (-jnp.arange(0, head_size, 2, dtype=jnp.float32) / head_size)
    angles = position * frequency[None, :]
    angles = jnp.concatenate([angles, angles], axis=-1)
    return (jnp.cos(angles)[:, None, :], jnp.sin(angles)[:, None, :])


def rotate(values, cosine, sine):
    half_size = values.shape[-1] // 2
    turned = jnp.concatenate([-values[..., half_size:], values[..., :half_size]], axis=-1)
    return values * cosine + turned * sine


def rotate_back(grads, cosine, sine):
    half_size = grads.shape[-1] // 2
    scaled = grads * sine
    return grads * cosine + jnp.concatenate(
        [scaled[..., half_size:], -scaled[..., :half_size]], axis=-1
    )


def transpose_dot(left, right):
    return lax.dot_general(
        left, right, (((1,), (1,)), ((), ())), preferred_element_type=jnp.float32
    )


def inner_rows(left, right):
    return lax.dot_general(
        left, right, (((0,), (0,)), ((), ())), preferred_element_type=jnp.float32
    )


def masked_scores(query, keys, allowed, scale):
    scores = jnp.einsum("lhe,mhe->hlm", query, keys, preferred_element_type=jnp.float32) * scale
    return jnp.where(allowed[None], scores, -1e30)


def attend(query, keys, values, allowed, scale):
    scores = masked_scores(query, keys, allowed, scale)
    highest = jnp.max(scores, axis=-1, keepdims=True)
    expo = jnp.exp(scores - highest)
    summed = jnp.sum(expo, axis=-1, keepdims=True)
    probs = (expo / summed).astype(jnp.bfloat16)
    output = jnp.einsum("hlm,mhe->lhe", probs, values, preferred_element_type=jnp.float32)
    return (output, highest + jnp.log(summed))


def attend_back(query, keys, values, log_total, grad_out, allowed, scale):
    probs = jnp.exp(masked_scores(query, keys, allowed, scale) - log_total)
    dprob = jnp.einsum("lhe,mhe->hlm", grad_out, values, preferred_element_type=jnp.float32)
    centre = jnp.sum(probs * dprob, axis=-1, keepdims=True)
    dscore = (probs * (dprob - centre)).astype(jnp.bfloat16)
    dquery = jnp.einsum("hlm,mhe->lhe", dscore, keys, preferred_element_type=jnp.float32) * scale
    dkeys = jnp.einsum("hlm,lhe->mhe", dscore, query, preferred_element_type=jnp.float32) * scale
    dvalues = jnp.einsum(
        "hlm,lhe->mhe", probs.astype(jnp.bfloat16), grad_out, preferred_element_type=jnp.float32
    )
    return (dquery, dkeys, dvalues)


def local(tokens, prefix, qkv_weight, out_weight, in_weight, down_weight, cotangent):
    micro = tokens.shape[0]
    length = tokens.shape[2]
    width = tokens.shape[3]
    hidden_units = down_weight.shape[0] * lax.axis_size("shard")
    scale = HD ** (-0.5)
    cosine, sine = rope_tables(length, HD)
    row_pos = lax.broadcasted_iota(jnp.int32, (length, length), 0)
    col_pos = lax.broadcasted_iota(jnp.int32, (length, length), 1)
    full_set = (
        lax.all_gather(qkv_weight, "shard", axis=0, tiled=True),
        lax.all_gather(out_weight, "shard", axis=0, tiled=True),
        lax.all_gather(in_weight, "shard", axis=0, tiled=True),
        lax.all_gather(down_weight, "shard", axis=0, tiled=True),
    )
    outputs = []
    grad_inputs = []
    kept_h1, kept_gqkv, kept_attn, kept_ga, kept_h2, kept_ggu, kept_hid, kept_gm = (
        [],
        [],
        [],
        [],
        [],
        [],
        [],
        [],
    )
    for batch_index in range(micro):
        xrow = tokens[batch_index, 0].astype(jnp.float32)
        normed_one, inverse_one = norm_rows(xrow)
        first_in = normed_one.astype(jnp.bfloat16)
        mixed = jnp.dot(first_in, full_set[0], preferred_element_type=jnp.float32)
        query = rotate(mixed[:, :width].reshape(length, H, HD), cosine, sine).astype(jnp.bfloat16)
        keys = rotate(mixed[:, width : 2 * width].reshape(length, H, HD), cosine, sine).astype(
            jnp.bfloat16
        )
        values = mixed[:, 2 * width :].reshape(length, H, HD).astype(jnp.bfloat16)
        allowed = (col_pos <= row_pos) | (col_pos < prefix[batch_index, 0])
        attended, log_total = attend(query, keys, values, allowed, scale)
        attn_low = attended.reshape(length, width).astype(jnp.bfloat16)
        middle = xrow + jnp.dot(attn_low, full_set[1], preferred_element_type=jnp.float32)
        normed_two, inverse_two = norm_rows(middle)
        second_in = normed_two.astype(jnp.bfloat16)
        gate_up = jnp.dot(second_in, full_set[2], preferred_element_type=jnp.float32)
        up_part = gate_up[:, :hidden_units]
        gate_part = gate_up[:, hidden_units:]
        sigmoid = jax.nn.sigmoid(gate_part)
        hidden = (gate_part * sigmoid * up_part).astype(jnp.bfloat16)
        final = middle + jnp.dot(hidden, full_set[3], preferred_element_type=jnp.float32)
        outputs.append(final.astype(jnp.bfloat16))
        grad_final = cotangent[batch_index, 0].astype(jnp.float32)
        grad_m = grad_final.astype(jnp.bfloat16)
        grad_hidden = transpose_dot(grad_m, full_set[3])
        grad_up = grad_hidden * (gate_part * sigmoid)
        grad_gate = grad_hidden * up_part * (sigmoid * (1.0 + gate_part * (1.0 - sigmoid)))
        grad_gu = jnp.concatenate([grad_up, grad_gate], axis=-1).astype(jnp.bfloat16)
        grad_mid = grad_final + norm_back(
            normed_two, inverse_two, transpose_dot(grad_gu, full_set[2])
        )
        grad_branch = grad_mid.astype(jnp.bfloat16)
        grad_att = transpose_dot(grad_branch, full_set[1]).astype(jnp.bfloat16)
        dquery, dkeys, dvalues = attend_back(
            query, keys, values, log_total, grad_att.reshape(length, H, HD), allowed, scale
        )
        dquery = rotate_back(dquery, cosine, sine).reshape(length, width)
        dkeys = rotate_back(dkeys, cosine, sine).reshape(length, width)
        grad_mixed = jnp.concatenate(
            [dquery, dkeys, dvalues.reshape(length, width)], axis=-1
        ).astype(jnp.bfloat16)
        grad_input = grad_mid + norm_back(
            normed_one, inverse_one, transpose_dot(grad_mixed, full_set[0])
        )
        grad_inputs.append(grad_input)
        kept_h1.append(first_in)
        kept_gqkv.append(grad_mixed)
        kept_attn.append(attn_low)
        kept_ga.append(grad_branch)
        kept_h2.append(second_in)
        kept_ggu.append(grad_gu)
        kept_hid.append(hidden)
        kept_gm.append(grad_m)
    all_h1 = jnp.concatenate(kept_h1, axis=0)
    all_gqkv = jnp.concatenate(kept_gqkv, axis=0)
    all_attn = jnp.concatenate(kept_attn, axis=0)
    all_ga = jnp.concatenate(kept_ga, axis=0)
    all_h2 = jnp.concatenate(kept_h2, axis=0)
    all_ggu = jnp.concatenate(kept_ggu, axis=0)
    all_hid = jnp.concatenate(kept_hid, axis=0)
    all_gm = jnp.concatenate(kept_gm, axis=0)
    part_one = inner_rows(all_h1, all_gqkv)
    part_two = inner_rows(all_attn, all_ga)
    part_three = inner_rows(all_h2, all_ggu)
    row_share = lax.psum_scatter(
        jnp.concatenate([part_one, part_two, part_three], axis=1),
        "shard",
        scatter_dimension=0,
        tiled=True,
    )
    down_share = lax.psum_scatter(
        inner_rows(all_hid, all_gm), "shard", scatter_dimension=0, tiled=True
    )
    grad_qkv, grad_out, grad_in, grad_down = (
        lax.psum(row_share[:, : 3 * width].astype(jnp.bfloat16), "rep").astype(jnp.float32),
        lax.psum(row_share[:, 3 * width : 4 * width].astype(jnp.bfloat16), "rep").astype(
            jnp.float32
        ),
        lax.psum(row_share[:, 4 * width :].astype(jnp.bfloat16), "rep").astype(jnp.float32),
        lax.psum(down_share.astype(jnp.bfloat16), "rep").astype(jnp.float32),
    )
    result = jnp.stack(outputs, axis=0)[:, None]
    grad_tokens = jnp.stack(grad_inputs, axis=0)[:, None]
    return (result, grad_tokens, grad_qkv, grad_out, grad_in, grad_down)


def solution(mesh):
    placed = (
        P(None, ("rep", "shard"), None, None),
        P(None, ("rep", "shard")),
        P("shard", None),
        P("shard", None),
        P("shard", None),
        P("shard", None),
        P(None, ("rep", "shard"), None, None),
    )
    return jax.shard_map(
        local,
        mesh=mesh,
        in_specs=placed,
        out_specs=(
            P(None, ("rep", "shard"), None, None),
            P(None, ("rep", "shard"), None, None),
            P("shard", None),
            P("shard", None),
            P("shard", None),
            P("shard", None),
        ),
        check_vma=False,
    )
```

profile of v0, /device:TPU:0, one launch (start us, length us, event | category | flops | bytes accessed | tf_op | source)
XLA Modules:
  0.0 870.6 jit_solution(7404513328902034223)
XLA Ops:
  17.9 57.0 %all-gather.5.cloned.1.call-done = bf16[1024,3072]{1,0:T(8,128)(2,1)} async-done(((bf16[64,3072]{1,0:T(8,128)(2,1)}), bf16[1024,3072]{1,0:T(8,128)(2,1)}) %all-gather.5.cloned.1.call-update) | async-done | bytes 6291472 | tf_op jit(solution)/shard_map/all_gather | solution.py:96
  74.9 4.0 fusion.154
  79.6 4.0 fusion.156
  87.9 29.1 %all-gather.7.cloned.1.call-done = bf16[1024,1024]{1,0:T(8,128)(2,1)} async-done(((bf16[64,1024]{1,0:T(8,128)(2,1)}), bf16[1024,1024]{1,0:T(8,128)(2,1)}) %all-gather.7.cloned.1.call-update) | async-done | bytes 2097168 | tf_op jit(solution)/shard_map/all_gather | solution.py:97
  117.0 2.3 fusion.153
  123.6 88.8 %all-gather.9.cloned.1.call-done = bf16[1024,5632]{1,0:T(8,128)(2,1)} async-done(((bf16[64,5632]{1,0:T(8,128)(2,1)}), bf16[1024,5632]{1,0:T(8,128)(2,1)}) %all-gather.9.cloned.1.call-update) | async-done | bytes 11534352 | tf_op jit(solution)/shard_map/all_gather | solution.py:98
  212.4 7.7 fusion.157
  220.2 3.3 fusion.155
  223.5 48.3 %all-gather.11.cloned.1.call-done = bf16[2816,1024]{1,0:T(8,128)(2,1)} async-done(((bf16[176,1024]{1,0:T(8,128)(2,1)}), bf16[2816,1024]{1,0:T(8,128)(2,1)}) %all-gather.11.cloned.1.call-update) | async-done | bytes 5767184 | tf_op jit(solution)/shard_map/all_gather | solution.py:99
  271.8 5.9 multiply_convert_fusion.1
  277.8 2.8 multiply_convert_fusion.3
  281.3 6.1 fusion.46
  289.0 8.9 %fusion.140 = (f32[64]{0:T(128)S(1)}, f32[64]{0:T(128)S(1)}, f32[64,1024]{1,0:T(8,128)S(1)}) fusion(f32[64]{0:T(128)} %copy-done.65, f32[64,1024]{1,0:T(8,128)} %copy-done.3, f32[64]{0:T(128)} %copy-done.57, bf16[1024,5632]{1,0:T(8,128)(2,1)} %all-gather.9.cloned.1.call-done, bf16[64,2816]{1,0:T(8,128)(2,1)} %get-tuple-element.35, ...), kind=kOutput, calls=%fused_computation.237 | convolution fusion | flops 739966848 | bytes 12780544 | tf_op jit(solution)/shard_map/dot_general | solution.py:47
  298.0 9.5 %fusion.139 = (f32[64]{0:T(128)S(1)}, f32[64]{0:T(128)S(1)}, f32[64,1024]{1,0:T(8,128)S(1)}) fusion(f32[64]{0:T(128)S(1)} %copy-done.64, f32[64,1024]{1,0:T(8,128)S(1)} %get-tuple-element.91, f32[64]{0:T(128)S(1)} %copy-done.56, bf16[1024,5632]{1,0:T(8,128)(2,1)} %all-gather.9.cloned.1.call-done, bf16[64,2816]{1,0:T(8,128)(2,1)S(1)} %copy-done.26, ...), kind=kOutput, calls=%fused_computation.236 | convolution fusion | flops 739966848 | bytes 12780544 | tf_op jit(solution)/shard_map/dot_general | solution.py:47
  321.8 6.5 fusion.26
  328.3 10.9 %fusion = f32[1024,5632]{1,0:T(8,128)} fusion(bf16[64,2816]{1,0:T(8,128)(2,1)S(1)} %copy-done.23, bf16[64,2816]{1,0:T(8,128)(2,1)S(1)} %copy-done.22, bf16[64,2816]{1,0:T(8,128)(2,1)S(1)} %copy-done.27, bf16[64,2816]{1,0:T(8,128)(2,1)S(1)} %copy-done.25, bf16[64,1024]{1,0:T(8,128)(2,1)S(1)} %copy-done.16, bf16[64,1024]{1,0:T(8,128)(2,1)S(1)} %fusion.122), kind=kOutput, calls=%fused_computation.1 | convolution fusion | flops 1482686464 | bytes 24772608 | tf_op jit(solution)/shard_map/dot_general | solution.py:53
  339.2 26.3 %pad_maximum_fusion = f32[1024,9728]{1,0:T(8,128)} fusion(f32[1024,5632]{1,0:T(8,128)} %fusion, f32[1024,1024]{1,0:T(8,128)S(1)} %fusion.97, f32[1024,3072]{1,0:T(8,128)} %fusion.26), kind=kLoop, calls=%fused_computation | loop fusion | flops 19922944 | bytes 79691776 | tf_op jit(solution)/shard_map/concatenate | solution.py:179
  366.6 3.9 fusion.12
  370.5 3.9 fusion.13
  375.1 4.8 fusion.20
  380.0 32.5 %reduce-scatter.5.cloned.1.call-done = f32[176,1024]{1,0:T(8,128)} async-done(((f32[2816,1024]{1,0:T(8,128)}), f32[176,1024]{1,0:T(8,128)}) %reduce-scatter.5.cloned.1.call-update) | async-done | bytes 720912 | tf_op jit(solution)/shard_map/reduce_scatter | solution.py:184
  414.4 386.4 %reduce-scatter.3.cloned.1.call-done = f32[64,9728]{1,0:T(8,128)} async-done(((f32[1024,9728]{1,0:T(8,128)}), f32[64,9728]{1,0:T(8,128)}) %reduce-scatter.3.cloned.1.call-update) | async-done | bytes 2490384 | tf_op jit(solution)/shard_map/reduce_scatter | solution.py:178
  805.1 5.0 fusion.138
  811.2 45.8 %all-reduce.3.cloned.1.call-done = (bf16[64,3072]{1,0:T(8,128)(2,1)}, bf16[64,1024]{1,0:T(8,128)(2,1)}, bf16[64,5632]{1,0:T(8,128)(2,1)}, bf16[176,1024]{1,0:T(8,128)(2,1)}) async-done(((bf16[64,3072]{1,0:T(8,128)(2,1)}, bf16[64,1024]{1,0:T(8,128)(2,1)}, bf16[64,5632]{1,0:T(8,128)(2,1)}, bf16[176,1024]{1,0:T(8,128)(2,1)}), (bf16[64,3072]{1,0:T(8,128)(2,1)}, bf16[64,1024]{1,0:T(8,128)(2,1)}, ...) | async-done | bytes 1605648 | tf_op jit(solution)/shard_map/psum | solution.py:188
  (236 shorter events, 51.7 us)
Async XLA Ops:
  7.2 10.5 %copy-start.6 = (bf16[2,1,64,1024]{3,2,1,0:T(8,128)(2,1)S(1)}, bf16[2,1,64,1024]{3,2,1,0:T(8,128)(2,1)}, u32[]{:S(2)}) copy-start(bf16[2,1,64,1024]{3,2,1,0:T(8,128)(2,1)} %param.7) | copy-start | bytes 786436
  7.2 67.7 %all-gather.5.cloned.1.call-start = ((), (), s32[]{:S(2)}) async-start(), calls=%async_computation.2 | async-start | bytes 6684672 | tf_op jit(solution)/shard_map/all_gather | solution.py:96
  7.9 109.1 %all-gather.7.cloned.1.call-start = ((), (), s32[]{:S(2)}) async-start(), calls=%async_computation.3 | async-start | bytes 2228224 | tf_op jit(solution)/shard_map/all_gather | solution.py:97
  8.7 203.8 %all-gather.9.cloned.1.call-start = ((), (), s32[]{:S(2)}) async-start(), calls=%async_computation.4 | async-start | bytes 12255232 | tf_op jit(solution)/shard_map/all_gather | solution.py:98
  9.4 262.4 %all-gather.11.cloned.1.call-start = ((), (), s32[]{:S(2)}) async-start(), calls=%async_computation.5 | async-start | bytes 6127616 | tf_op jit(solution)/shard_map/all_gather | solution.py:99
  10.0 402.5 %reduce-scatter.5.cloned.1.call-start = ((), (), s32[]{:S(2)}) async-start(), calls=%async_computation.7 | async-start | bytes 12255232 | tf_op jit(solution)/shard_map/reduce_scatter | solution.py:184
  14.6 60.3 %copy-start.51 = (f32[64]{0:T(128)}, f32[64]{0:T(128)S(1)}, u32[]{:S(2)}) copy-start(f32[64]{0:T(128)S(1)} %get-tuple-element.100) | copy-start | bytes 772
  14.6 60.3 %copy-start.53 = (f32[64]{0:T(128)}, f32[64]{0:T(128)S(1)}, u32[]{:S(2)}) copy-start(f32[64]{0:T(128)S(1)} %get-tuple-element.101) | copy-start | bytes 772
  15.8 59.1 %copy-start.59 = (f32[64]{0:T(128)}, f32[64]{0:T(128)S(1)}, u32[]{:S(2)}) copy-start(f32[64]{0:T(128)S(1)} %add_rsqrt_fusion.3) | copy-start | bytes 772
  15.8 59.1 %copy-start.61 = (f32[64]{0:T(128)}, f32[64]{0:T(128)S(1)}, u32[]{:S(2)}) copy-start(f32[64]{0:T(128)S(1)} %add_rsqrt_fusion.1) | copy-start | bytes 772
  17.9 61.0 %copy-start.28 = (bf16[64,1024]{1,0:T(8,128)(2,1)}, bf16[64,1024]{1,0:T(8,128)(2,1)S(1)}, u32[]{:S(2)}) copy-start(bf16[64,1024]{1,0:T(8,128)(2,1)S(1)} %get-tuple-element.64) | copy-start | bytes 393220
  17.9 61.7 %copy-start.30 = (bf16[64,1024]{1,0:T(8,128)(2,1)}, bf16[64,1024]{1,0:T(8,128)(2,1)S(1)}, u32[]{:S(2)}) copy-start(bf16[64,1024]{1,0:T(8,128)(2,1)S(1)} %get-tuple-element.65) | copy-start | bytes 393220
  87.6 32.0 %copy-start.49 = (f32[16,64]{1,0:T(8,128)}, f32[16,64]{1,0:T(8,128)S(1)}, u32[]{:S(2)}) copy-start(f32[16,64]{1,0:T(8,128)S(1)} %fusion.64) | copy-start | bytes 12292
  87.9 31.7 %copy-start.33 = (bf16[16,64,64]{2,1,0:T(8,128)(2,1)}, bf16[16,64,64]{2,1,0:T(8,128)(2,1)S(1)}, u32[]{:S(2)}) copy-start(bf16[16,64,64]{2,1,0:T(8,128)(2,1)S(1)} %convolution_convert_fusion.3) | copy-start | bytes 393220
  287.5 513.3 %reduce-scatter.3.cloned.1.call-start = ((), (), s32[]{:S(2)}) async-start(), calls=%async_computation.6 | async-start | bytes 42336256 | tf_op jit(solution)/shard_map/reduce_scatter | solution.py:178
  289.0 9.0 %copy-start.24 = (bf16[64,2816]{1,0:T(8,128)(2,1)S(1)}, bf16[64,2816]{1,0:T(8,128)(2,1)}, u32[]{:S(2)}) copy-start(bf16[64,2816]{1,0:T(8,128)(2,1)} %get-tuple-element.32) | copy-start | bytes 1081348
  289.0 9.0 %copy-start.26 = (bf16[64,2816]{1,0:T(8,128)(2,1)S(1)}, bf16[64,2816]{1,0:T(8,128)(2,1)}, u32[]{:S(2)}) copy-start(bf16[64,2816]{1,0:T(8,128)(2,1)} %get-tuple-element.33) | copy-start | bytes 1081348
  289.0 9.0 %copy-start.56 = (f32[64]{0:T(128)S(1)}, f32[64]{0:T(128)}, u32[]{:S(2)}) copy-start(f32[64]{0:T(128)} %copy-done.55) | copy-start | bytes 772
  289.0 9.0 %copy-start.64 = (f32[64]{0:T(128)S(1)}, f32[64]{0:T(128)}, u32[]{:S(2)}) copy-start(f32[64]{0:T(128)} %copy-done.63) | copy-start | bytes 772
  298.0 9.6 %copy-start.4 = (f32[64,1024]{1,0:T(8,128)S(1)}, f32[64,1024]{1,0:T(8,128)}, u32[]{:S(2)}) copy-start(f32[64,1024]{1,0:T(8,128)} %copy-done.3) | copy-start | bytes 786436
  298.0 9.6 %copy-start.42 = (bf16[2,1,64,1024]{3,2,1,0:T(8,128)(2,1)S(1)}, bf16[2,1,64,1024]{3,2,1,0:T(8,128)(2,1)}, u32[]{:S(2)}) copy-start(bf16[2,1,64,1024]{3,2,1,0:T(8,128)(2,1)} %param.13) | copy-start | bytes 786436
  298.0 9.6 %copy-start.58 = (f32[64]{0:T(128)S(1)}, f32[64]{0:T(128)}, u32[]{:S(2)}) copy-start(f32[64]{0:T(128)} %copy-done.57) | copy-start | bytes 772
  298.0 9.6 %copy-start.66 = (f32[64]{0:T(128)S(1)}, f32[64]{0:T(128)}, u32[]{:S(2)}) copy-start(f32[64]{0:T(128)} %copy-done.65) | copy-start | bytes 772
  365.6 491.5 %all-reduce.3.cloned.1.call-start = ((), (), s32[]{:S(2)}) async-start(), calls=%async_computation.8 | async-start | bytes 3211264 | tf_op jit(solution)/shard_map/psum | solution.py:188
  (50 other events, 153.2 us)
Sparse Core Ops, SparseCore 0:
  10.3 64.5 all-gather.4
  77.0 39.9 all-gather.6
  119.3 93.0 all-gather.8
  214.6 57.1 all-gather.10
  287.6 124.8 reduce-scatter.4
  417.3 383.4 reduce-scatter.2
  805.1 51.8 all-reduce.2
where the time goes:
time: 871 us
  waiting for transfers between devices  690 us (79%)
  matrix products  100 us (11%)
  other arithmetic  49.7 us (6%)
  between operations  15.2 us (2%)
  local copies, waits for them, and re-layouts  14.9 us (2%)
    reduce_scatter x1, waiting for transfers between devices, local(): lax.psum_scatter(jnp.concatenate([part_one, part_two, part_three], axis=1...  386 us
    all_gather x1, waiting for transfers between devices, local(): lax.all_gather(in_weight, 'shard', axis=0, tiled=True)  88.8 us
    all_gather x1, waiting for transfers between devices, local(): lax.all_gather(qkv_weight, 'shard', axis=0, tiled=True)  57 us
    all_gather x1, waiting for transfers between devices, local(): lax.all_gather(down_weight, 'shard', axis=0, tiled=True)  48.3 us
    psum x1, waiting for transfers between devices, local(): lax.psum(row_share[:, :3 * width].astype(jnp.bfloat16), 'rep')  45.8 us
    dot_general x8, matrix products, transpose_dot(): lax.dot_general(left, right, (((1,), (1,)), ((), ())), preferred_element_...  40.7 us
    reduce_scatter x1, waiting for transfers between devices, local(): lax.psum_scatter(inner_rows(all_hid, all_gm), 'shard', scatter_dimension=...  32.5 us
    all_gather x1, waiting for transfers between devices, local(): lax.all_gather(out_weight, 'shard', axis=0, tiled=True)  29.1 us
  transfers between devices with their start and end apart: 7, of which 7 were waited for; matrix products, arithmetic and copies ran while one was open for 15% of the time, Pallas kernels for 0%

commit v1 on v0

--- a/solution.py
+++ b/solution.py
@@ -5,6 +5,17 @@
 
 H = 16
 HD = 64
+
+
+def collect(x, axis, dim):
+    ways = lax.axis_size(axis)
+    pieces = [x]
+    for far in range(1, ways):
+        pieces.append(
+            lax.ppermute(pieces[far - 1], axis, [(d, (d - 1) % ways) for d in range(ways)])
+        )
+    line = jnp.concatenate(pieces, axis=dim)
+    return jnp.roll(line, lax.axis_index(axis) * x.shape[dim], axis=dim)
 
 
 def norm_rows(values):
@@ -93,7 +104,7 @@
     row_pos = lax.broadcasted_iota(jnp.int32, (length, length), 0)
     col_pos = lax.broadcasted_iota(jnp.int32, (length, length), 1)
     full_set = (
-        lax.all_gather(qkv_weight, "shard", axis=0, tiled=True),
+        collect(qkv_weight, "shard", 0),
         lax.all_gather(out_weight, "shard", axis=0, tiled=True),
         lax.all_gather(in_weight, "shard", axis=0, tiled=True),
         lax.all_gather(down_weight, "shard", axis=0, tiled=True),

time: 871 us -> 869 us (level)
  waiting for transfers between devices: 690 us -> 608 us
  starting transfers between devices: 0.27 us -> 70.4 us
    ppermute x0 -> x15, waiting for transfers between devices: none -> 138 us  [collect(): lax.ppermute(pieces[far - 1], axis, [(d, (d - 1) % ways) for d in range(w...]
    all_gather x1, waiting for transfers between devices: 88.8 us -> 0.02 us  [local(): lax.all_gather(in_weight, 'shard', axis=0, tiled=True)]
    ppermute x0 -> x15, starting transfers between devices: none -> 70.2 us  [collect(): lax.ppermute(pieces[far - 1], axis, [(d, (d - 1) % ways) for d in range(w...]
    all_gather x1 -> x0, waiting for transfers between devices: 57 us -> none  [local(): lax.all_gather(qkv_weight, 'shard', axis=0, tiled=True)]
    all_gather x1, waiting for transfers between devices: 48.3 us -> 0.02 us  [local(): lax.all_gather(down_weight, 'shard', axis=0, tiled=True)]
    all_gather x1, waiting for transfers between devices: 29.1 us -> 0.02 us  [local(): lax.all_gather(out_weight, 'shard', axis=0, tiled=True)]
  transfers between devices with their start and end apart: 7 -> 21, of which waited for: 7 -> 18; matrix products, arithmetic and copies ran while one was open for 15% -> 16% of each run, Pallas kernels for 0% -> 0%
where the time goes in v1:
time: 869 us; the launch traced here: 868 us
  waiting for transfers between devices  608 us (70%)
  matrix products  105 us (12%)
  starting transfers between devices  70.4 us (8%)
  other arithmetic  49.5 us (6%)
  local copies, waits for them, and re-layouts  19.5 us (2%)
  between operations  15.4 us (2%)
    reduce_scatter x1, waiting for transfers between devices, local(): lax.psum_scatter(jnp.concatenate([part_one, part_two, part_three], axis=1...  386 us
    ppermute x15, waiting for transfers between devices, collect(): lax.ppermute(pieces[far - 1], axis, [(d, (d - 1) % ways) for d in range(w...  138 us
    ppermute x15, starting transfers between devices, collect(): lax.ppermute(pieces[far - 1], axis, [(d, (d - 1) % ways) for d in range(w...  70.2 us
    psum x1, waiting for transfers between devices, local(): lax.psum(row_share[:, :3 * width].astype(jnp.bfloat16), 'rep')  45.2 us
    dot_general x8, matrix products, transpose_dot(): lax.dot_general(left, right, (((1,), (1,)), ((), ())), preferred_element_...  43.4 us
    reduce_scatter x1, waiting for transfers between devices, local(): lax.psum_scatter(inner_rows(all_hid, all_gm), 'shard', scatter_dimension=...  36.9 us
    dot_general x4, matrix products, inner_rows(): lax.dot_general(left, right, (((0,), (0,)), ((), ())), preferred_element_...  25.4 us
    concatenate x1, other arithmetic, local(): jnp.concatenate([part_one, part_two, part_three], axis=1)  24.9 us
  transfers between devices with their start and end apart: 21, of which 18 were waited for; matrix products, arithmetic and copies ran while one was open for 16% of the time, Pallas kernels for 0%

profile of v1, /device:TPU:0, one launch (start us, length us, event | category | flops | bytes accessed | tf_op | source)
XLA Modules:
  0.0 868.2 jit_solution(12692442344748588357)
XLA Ops:
  14.2 5.6 collective-permute-done
  26.4 5.9 collective-permute-done.1
  38.7 8.4 collective-permute-done.2
  73.4 12.0 %collective-permute-done.5 = bf16[64,3072]{1,0:T(8,128)(2,1)S(1)} collective-permute-done((bf16[64,3072]{1,0:T(8,128)(2,1)S(1)}, bf16[64,3072]{1,0:T(8,128)(2,1)S(1)}, u32[]{:S(2)}, u32[]{:S(2)}) %collective-permute-start.5) | collective-permute-done | bytes 393248 | tf_op jit(solution)/shard_map/ppermute | solution.py:15
  92.0 7.7 collective-permute-done.6
  106.3 11.3 %collective-permute-done.7 = bf16[64,3072]{1,0:T(8,128)(2,1)S(1)} collective-permute-done((bf16[64,3072]{1,0:T(8,128)(2,1)S(1)}, bf16[64,3072]{1,0:T(8,128)(2,1)S(1)}, u32[]{:S(2)}, u32[]{:S(2)}) %collective-permute-start.7) | collective-permute-done | bytes 393248 | tf_op jit(solution)/shard_map/ppermute | solution.py:15
  122.3 13.6 %collective-permute-done.8 = bf16[64,3072]{1,0:T(8,128)(2,1)S(1)} collective-permute-done((bf16[64,3072]{1,0:T(8,128)(2,1)S(1)}, bf16[64,3072]{1,0:T(8,128)(2,1)S(1)}, u32[]{:S(2)}, u32[]{:S(2)}) %collective-permute-start.8) | collective-permute-done | bytes 393248 | tf_op jit(solution)/shard_map/ppermute | solution.py:15
  140.6 12.1 %collective-permute-done.9 = bf16[64,3072]{1,0:T(8,128)(2,1)S(1)} collective-permute-done((bf16[64,3072]{1,0:T(8,128)(2,1)S(1)}, bf16[64,3072]{1,0:T(8,128)(2,1)S(1)}, u32[]{:S(2)}, u32[]{:S(2)}) %collective-permute-start.9) | collective-permute-done | bytes 393248 | tf_op jit(solution)/shard_map/ppermute | solution.py:15
  157.4 11.4 %collective-permute-done.10 = bf16[64,3072]{1,0:T(8,128)(2,1)S(1)} collective-permute-done((bf16[64,3072]{1,0:T(8,128)(2,1)S(1)}, bf16[64,3072]{1,0:T(8,128)(2,1)S(1)}, u32[]{:S(2)}, u32[]{:S(2)}) %collective-permute-start.10) | collective-permute-done | bytes 393248 | tf_op jit(solution)/shard_map/ppermute | solution.py:15
  183.4 13.6 %collective-permute-done.12 = bf16[64,3072]{1,0:T(8,128)(2,1)S(1)} collective-permute-done((bf16[64,3072]{1,0:T(8,128)(2,1)S(1)}, bf16[64,3072]{1,0:T(8,128)(2,1)S(1)}, u32[]{:S(2)}, u32[]{:S(2)}) %collective-permute-start.12) | collective-permute-done | bytes 393248 | tf_op jit(solution)/shard_map/ppermute | solution.py:15
  201.7 9.1 %collective-permute-done.13 = bf16[64,3072]{1,0:T(8,128)(2,1)S(1)} collective-permute-done((bf16[64,3072]{1,0:T(8,128)(2,1)S(1)}, bf16[64,3072]{1,0:T(8,128)(2,1)S(1)}, u32[]{:S(2)}, u32[]{:S(2)}) %collective-permute-start.13) | collective-permute-done | bytes 393248 | tf_op jit(solution)/shard_map/ppermute | solution.py:15
  215.5 13.7 %collective-permute-done.14 = bf16[64,3072]{1,0:T(8,128)(2,1)S(1)} collective-permute-done((bf16[64,3072]{1,0:T(8,128)(2,1)S(1)}, bf16[64,3072]{1,0:T(8,128)(2,1)S(1)}, u32[]{:S(2)}, u32[]{:S(2)}) %collective-permute-start.14) | collective-permute-done | bytes 393248 | tf_op jit(solution)/shard_map/ppermute | solution.py:15
  253.1 7.6 fusion.165
  262.9 5.8 multiply_convert_fusion.1
  268.7 5.6 multiply_convert_fusion.3
  275.0 6.1 fusion.52
  281.4 8.3 fusion.150
  289.7 9.9 %fusion.149 = (f32[64]{0:T(128)S(1)}, f32[64]{0:T(128)S(1)}, f32[64,1024]{1,0:T(8,128)S(1)}) fusion(f32[64]{0:T(128)} %copy-done.53, f32[64,1024]{1,0:T(8,128)S(1)} %get-tuple-element.91, f32[64]{0:T(128)} %copy-done.45, bf16[1024,5632]{1,0:T(8,128)(2,1)} %all-gather.6.cloned.1.call-done, bf16[64,2816]{1,0:T(8,128)(2,1)} %get-tuple-element.33, ...), kind=kOutput, calls=%fused_computation.278 | convolution fusion | flops 739966848 | bytes 12780544 | tf_op jit(solution)/shard_map/dot_general | solution.py:58
  317.1 6.4 fusion.32
  323.5 11.0 %fusion.8 = f32[1024,5632]{1,0:T(8,128)} fusion(bf16[64,2816]{1,0:T(8,128)(2,1)S(1)} %copy-done.21, bf16[64,2816]{1,0:T(8,128)(2,1)S(1)} %copy-done.20, bf16[64,2816]{1,0:T(8,128)(2,1)S(1)} %copy-done.23, bf16[64,2816]{1,0:T(8,128)(2,1)S(1)} %copy-done.22, bf16[64,1024]{1,0:T(8,128)(2,1)S(1)} %copy-done.14, bf16[64,1024]{1,0:T(8,128)(2,1)S(1)} %fusion.128), kind=kOutput, calls=%fused_computation.9 | convolution fusion | flops 1482686464 | bytes 24772608 | tf_op jit(solution)/shard_map/dot_general | solution.py:64
  334.5 24.9 %pad_maximum_fusion = f32[1024,9728]{1,0:T(8,128)} fusion(f32[1024,5632]{1,0:T(8,128)} %fusion.8, f32[1024,1024]{1,0:T(8,128)S(1)} %fusion.103, f32[1024,3072]{1,0:T(8,128)} %fusion.32), kind=kLoop, calls=%fused_computation | loop fusion | flops 19922944 | bytes 79691776 | tf_op jit(solution)/shard_map/concatenate | solution.py:190
  372.3 36.9 %reduce-scatter.5.cloned.1.call-done = f32[176,1024]{1,0:T(8,128)} async-done(((f32[2816,1024]{1,0:T(8,128)}), f32[176,1024]{1,0:T(8,128)}) %reduce-scatter.5.cloned.1.call-update) | async-done | bytes 720912 | tf_op jit(solution)/shard_map/reduce_scatter | solution.py:195
  411.1 386.3 %reduce-scatter.3.cloned.1.call-done = f32[64,9728]{1,0:T(8,128)} async-done(((f32[1024,9728]{1,0:T(8,128)}), f32[64,9728]{1,0:T(8,128)}) %reduce-scatter.3.cloned.1.call-update) | async-done | bytes 2490384 | tf_op jit(solution)/shard_map/reduce_scatter | solution.py:189
  808.4 45.2 %all-reduce.3.cloned.1.call-done = (bf16[64,3072]{1,0:T(8,128)(2,1)}, bf16[64,1024]{1,0:T(8,128)(2,1)}, bf16[64,5632]{1,0:T(8,128)(2,1)}, bf16[176,1024]{1,0:T(8,128)(2,1)}) async-done(((bf16[64,3072]{1,0:T(8,128)(2,1)}, bf16[64,1024]{1,0:T(8,128)(2,1)}, bf16[64,5632]{1,0:T(8,128)(2,1)}, bf16[176,1024]{1,0:T(8,128)(2,1)}), (bf16[64,3072]{1,0:T(8,128)(2,1)}, bf16[64,1024]{1,0:T(8,128)(2,1)}, ...) | async-done | bytes 1605648 | tf_op jit(solution)/shard_map/psum | solution.py:199
  (275 shorter events, 174.3 us)
Async XLA Ops:
  7.2 237.5 %all-gather.4.cloned.1.call-start = ((), (), s32[]{:S(2)}) async-start(), calls=%async_computation.2 | async-start | bytes 2228224 | tf_op jit(solution)/shard_map/all_gather | solution.py:108
  7.9 245.1 %all-gather.6.cloned.1.call-start = ((), (), s32[]{:S(2)}) async-start(), calls=%async_computation.3 | async-start | bytes 12255232 | tf_op jit(solution)/shard_map/all_gather | solution.py:109
  8.7 254.2 %all-gather.8.cloned.1.call-start = ((), (), s32[]{:S(2)}) async-start(), calls=%async_computation.4 | async-start | bytes 6127616 | tf_op jit(solution)/shard_map/all_gather | solution.py:110
  8.7 11.1 %collective-permute-start = (bf16[64,3072]{1,0:T(8,128)(2,1)}, bf16[64,3072]{1,0:T(8,128)(2,1)S(1)}, u32[]{:S(2)}, u32[]{:S(2)}) collective-permute-start(bf16[64,3072]{1,0:T(8,128)(2,1)} %param.9), channel_id=1, source_target_pairs={{0,15},{1,0},{2,1},{3,2},{4,3},{5,4},{6,5},{7,6},{8,7},{9,8},{10,9... | collective-permute-start | bytes 1179656 | tf_op jit(solution)/shard_map/ppermute | solution.py:15
  19.8 12.4 %collective-permute-start.1 = (bf16[64,3072]{1,0:T(8,128)(2,1)S(1)}, bf16[64,3072]{1,0:T(8,128)(2,1)S(1)}, u32[]{:S(2)}, u32[]{:S(2)}) collective-permute-start(bf16[64,3072]{1,0:T(8,128)(2,1)S(1)} %collective-permute-done), channel_id=1, source_target_pairs={{0,15},{1,0},{2,1},{3,2},{4,3},{5,4},{6,5},{7,6},{8,7},{9,8},{10,9... | collective-permute-start | bytes 1179656 | tf_op jit(solution)/shard_map/ppermute | solution.py:15
  24.3 384.9 %reduce-scatter.5.cloned.1.call-start = ((), (), s32[]{:S(2)}) async-start(), calls=%async_computation.6 | async-start | bytes 12255232 | tf_op jit(solution)/shard_map/reduce_scatter | solution.py:195
  32.2 14.8 %collective-permute-start.2 = (bf16[64,3072]{1,0:T(8,128)(2,1)S(1)}, bf16[64,3072]{1,0:T(8,128)(2,1)S(1)}, u32[]{:S(2)}, u32[]{:S(2)}) collective-permute-start(bf16[64,3072]{1,0:T(8,128)(2,1)S(1)} %collective-permute-done.1), channel_id=1, source_target_pairs={{0,15},{1,0},{2,1},{3,2},{4,3},{5,4},{6,5},{7,6},{8,7},{9,8},{10,9... | collective-permute-start | bytes 1179656 | tf_op jit(solution)/shard_map/ppermute | solution.py:15
  47.1 10.1 %collective-permute-start.3 = (bf16[64,3072]{1,0:T(8,128)(2,1)S(1)}, bf16[64,3072]{1,0:T(8,128)(2,1)S(1)}, u32[]{:S(2)}, u32[]{:S(2)}) collective-permute-start(bf16[64,3072]{1,0:T(8,128)(2,1)S(1)} %collective-permute-done.2), channel_id=1, source_target_pairs={{0,15},{1,0},{2,1},{3,2},{4,3},{5,4},{6,5},{7,6},{8,7},{9,8},{10,9... | collective-permute-start | bytes 1179656 | tf_op jit(solution)/shard_map/ppermute | solution.py:15
  57.2 9.9 %collective-permute-start.4 = (bf16[64,3072]{1,0:T(8,128)(2,1)S(1)}, bf16[64,3072]{1,0:T(8,128)(2,1)S(1)}, u32[]{:S(2)}, u32[]{:S(2)}) collective-permute-start(bf16[64,3072]{1,0:T(8,128)(2,1)S(1)} %collective-permute-done.3), channel_id=1, source_target_pairs={{0,15},{1,0},{2,1},{3,2},{4,3},{5,4},{6,5},{7,6},{8,7},{9,8},{10,9... | collective-permute-start | bytes 1179656 | tf_op jit(solution)/shard_map/ppermute | solution.py:15
  67.1 18.3 %collective-permute-start.5 = (bf16[64,3072]{1,0:T(8,128)(2,1)S(1)}, bf16[64,3072]{1,0:T(8,128)(2,1)S(1)}, u32[]{:S(2)}, u32[]{:S(2)}) collective-permute-start(bf16[64,3072]{1,0:T(8,128)(2,1)S(1)} %collective-permute-done.4), channel_id=1, source_target_pairs={{0,15},{1,0},{2,1},{3,2},{4,3},{5,4},{6,5},{7,6},{8,7},{9,8},{10,9... | collective-permute-start | bytes 1179656 | tf_op jit(solution)/shard_map/ppermute | solution.py:15
  85.4 14.3 %collective-permute-start.6 = (bf16[64,3072]{1,0:T(8,128)(2,1)S(1)}, bf16[64,3072]{1,0:T(8,128)(2,1)S(1)}, u32[]{:S(2)}, u32[]{:S(2)}) collective-permute-start(bf16[64,3072]{1,0:T(8,128)(2,1)S(1)} %collective-permute-done.5), channel_id=1, source_target_pairs={{0,15},{1,0},{2,1},{3,2},{4,3},{5,4},{6,5},{7,6},{8,7},{9,8},{10,9... | collective-permute-start | bytes 1179656 | tf_op jit(solution)/shard_map/ppermute | solution.py:15
  99.7 17.9 %collective-permute-start.7 = (bf16[64,3072]{1,0:T(8,128)(2,1)S(1)}, bf16[64,3072]{1,0:T(8,128)(2,1)S(1)}, u32[]{:S(2)}, u32[]{:S(2)}) collective-permute-start(bf16[64,3072]{1,0:T(8,128)(2,1)S(1)} %collective-permute-done.6), channel_id=1, source_target_pairs={{0,15},{1,0},{2,1},{3,2},{4,3},{5,4},{6,5},{7,6},{8,7},{9,8},{10,9... | collective-permute-start | bytes 1179656 | tf_op jit(solution)/shard_map/ppermute | solution.py:15
  117.6 18.3 %collective-permute-start.8 = (bf16[64,3072]{1,0:T(8,128)(2,1)S(1)}, bf16[64,3072]{1,0:T(8,128)(2,1)S(1)}, u32[]{:S(2)}, u32[]{:S(2)}) collective-permute-start(bf16[64,3072]{1,0:T(8,128)(2,1)S(1)} %collective-permute-done.7), channel_id=1, source_target_pairs={{0,15},{1,0},{2,1},{3,2},{4,3},{5,4},{6,5},{7,6},{8,7},{9,8},{10,9... | collective-permute-start | bytes 1179656 | tf_op jit(solution)/shard_map/ppermute | solution.py:15
  135.9 16.8 %collective-permute-start.9 = (bf16[64,3072]{1,0:T(8,128)(2,1)S(1)}, bf16[64,3072]{1,0:T(8,128)(2,1)S(1)}, u32[]{:S(2)}, u32[]{:S(2)}) collective-permute-start(bf16[64,3072]{1,0:T(8,128)(2,1)S(1)} %collective-permute-done.8), channel_id=1, source_target_pairs={{0,15},{1,0},{2,1},{3,2},{4,3},{5,4},{6,5},{7,6},{8,7},{9,8},{10,9... | collective-permute-start | bytes 1179656 | tf_op jit(solution)/shard_map/ppermute | solution.py:15
  152.7 16.2 %collective-permute-start.10 = (bf16[64,3072]{1,0:T(8,128)(2,1)S(1)}, bf16[64,3072]{1,0:T(8,128)(2,1)S(1)}, u32[]{:S(2)}, u32[]{:S(2)}) collective-permute-start(bf16[64,3072]{1,0:T(8,128)(2,1)S(1)} %collective-permute-done.9), channel_id=1, source_target_pairs={{0,15},{1,0},{2,1},{3,2},{4,3},{5,4},{6,5},{7,6},{8,7},{9,8},{10,9... | collective-permute-start | bytes 1179656 | tf_op jit(solution)/shard_map/ppermute | solution.py:15
  168.9 9.9 %collective-permute-start.11 = (bf16[64,3072]{1,0:T(8,128)(2,1)S(1)}, bf16[64,3072]{1,0:T(8,128)(2,1)S(1)}, u32[]{:S(2)}, u32[]{:S(2)}) collective-permute-start(bf16[64,3072]{1,0:T(8,128)(2,1)S(1)} %collective-permute-done.10), channel_id=1, source_target_pairs={{0,15},{1,0},{2,1},{3,2},{4,3},{5,4},{6,5},{7,6},{8,7},{9,8},{10,9... | collective-permute-start | bytes 1179656 | tf_op jit(solution)/shard_map/ppermute | solution.py:15
  178.8 18.2 %collective-permute-start.12 = (bf16[64,3072]{1,0:T(8,128)(2,1)S(1)}, bf16[64,3072]{1,0:T(8,128)(2,1)S(1)}, u32[]{:S(2)}, u32[]{:S(2)}) collective-permute-start(bf16[64,3072]{1,0:T(8,128)(2,1)S(1)} %collective-permute-done.11), channel_id=1, source_target_pairs={{0,15},{1,0},{2,1},{3,2},{4,3},{5,4},{6,5},{7,6},{8,7},{9,8},{10,9... | collective-permute-start | bytes 1179656 | tf_op jit(solution)/shard_map/ppermute | solution.py:15
  197.0 13.8 %collective-permute-start.13 = (bf16[64,3072]{1,0:T(8,128)(2,1)S(1)}, bf16[64,3072]{1,0:T(8,128)(2,1)S(1)}, u32[]{:S(2)}, u32[]{:S(2)}) collective-permute-start(bf16[64,3072]{1,0:T(8,128)(2,1)S(1)} %collective-permute-done.12), channel_id=1, source_target_pairs={{0,15},{1,0},{2,1},{3,2},{4,3},{5,4},{6,5},{7,6},{8,7},{9,8},{10,9... | collective-permute-start | bytes 1179656 | tf_op jit(solution)/shard_map/ppermute | solution.py:15
  210.8 18.4 %collective-permute-start.14 = (bf16[64,3072]{1,0:T(8,128)(2,1)S(1)}, bf16[64,3072]{1,0:T(8,128)(2,1)S(1)}, u32[]{:S(2)}, u32[]{:S(2)}) collective-permute-start(bf16[64,3072]{1,0:T(8,128)(2,1)S(1)} %collective-permute-done.13), channel_id=1, source_target_pairs={{0,15},{1,0},{2,1},{3,2},{4,3},{5,4},{6,5},{7,6},{8,7},{9,8},{10,9... | collective-permute-start | bytes 1179656 | tf_op jit(solution)/shard_map/ppermute | solution.py:15
  281.2 516.2 %reduce-scatter.3.cloned.1.call-start = ((), (), s32[]{:S(2)}) async-start(), calls=%async_computation.5 | async-start | bytes 42336256 | tf_op jit(solution)/shard_map/reduce_scatter | solution.py:189
  359.5 494.2 %all-reduce.3.cloned.1.call-start = ((), (), s32[]{:S(2)}) async-start(), calls=%async_computation.7 | async-start | bytes 3211264 | tf_op jit(solution)/shard_map/psum | solution.py:199
  364.6 437.7 %copy-start.7 = (bf16[2,1,64,1024]{3,2,1,0:T(8,128)(2,1)S(1)}, bf16[2,1,64,1024]{3,2,1,0:T(8,128)(2,1)}, u32[]{:S(2)}) copy-start(bf16[2,1,64,1024]{3,2,1,0:T(8,128)(2,1)} %param.7) | copy-start | bytes 786436
  368.4 438.9 %copy-start.31 = (f32[64,1024]{1,0:T(8,128)S(1)}, f32[64,1024]{1,0:T(8,128)}, u32[]{:S(2)}) copy-start(f32[64,1024]{1,0:T(8,128)} %get-tuple-element.29) | copy-start | bytes 786436
  368.4 438.9 %copy-start.32 = (f32[64,1024]{1,0:T(8,128)S(1)}, f32[64,1024]{1,0:T(8,128)}, u32[]{:S(2)}) copy-start(f32[64,1024]{1,0:T(8,128)} %get-tuple-element.63) | copy-start | bytes 786436
  (54 other events, 2579.8 us)
Sparse Core Ops, SparseCore 0:
  10.2 46.3 all-gather.3
  58.8 111.0 all-gather.5
  172.2 62.9 all-gather.7
  281.3 127.8 reduce-scatter.4
  414.0 383.3 reduce-scatter.2
  801.7 51.8 all-reduce.2
